TPU v7x, 32 devices: a whole 2x2x4 slice. The times are simulated.
32 devices in a mesh: grp: 2 (over y), pol: 16 (over z, x, core).
Axes of the slice: x: 2, y: 2, z: 4, core: 2. Of those that a mesh axis runs over, the one named last changes fastest.
Arguments:
- shocks: float32 [6, 128, 1024], P('grp'), parts along dimension 0, may hold values from -6 to 6
- loadings: float32 [1024, 128], P('pol'), may hold values from -0.5 to 0.5
- sec_drift: float32 [1024], P('pol'), may hold values from -0.02 to 0.08
- holdings: float32 [1024, 128], P('pol'), may hold values from -0.1875 to 0.1875
- fund_of: int32 [8192, 1], P('pol'), may hold values from 0 to 127
- product_type: int32 [8192], P('pol'), may hold values from 0 to 7
- term_years: int32 [8192], P('pol'), may hold values from 1 to 3
- asset_start: float32 [8192], P('pol'), may hold values from 0.35 to 3
- liab_start: float32 [8192], P('pol'), may hold values from 0.3 to 3
- base_lapse: float32 [8], replicated, may hold values from 0.02 to 0.2
- guarantee: float32 [8], replicated, may hold values from 0 to 0.08
- lapse_draw: bfloat16 [8192, 6, 1024], P('pol', 'grp'), parts along dimension 1, may hold values from 0 to 1
Outputs:
- assets: float32 [8192, 2048], P('pol', 'grp'), parts along dimension 1
- liability: float32 [8192, 2048], P('pol', 'grp'), parts along dimension 1
- credit_rates: float32 [6, 128, 1024], P('grp', None, 'pol'), parts along dimension 0
There are 2 independent parts, one for each index of `grp`. A program takes and returns all parts, laid end to end along the dimension named above; an argument that names none is the same for every part. Nothing has to cross between parts.
Inputs may be any that keep to these rules, and one draw needn't show every extreme that they name: `fund_of`: every fund backs at least one policy.
All inputs are finite; a program needn't handle non-finite values.
Results may differ from a plain program's by a relative error of at most 0.0003.
Values sent between devices are 32-bit elements; how exact they have to be, the bound alone decides.
A program may use at most 64 MiB of HBM per device.

v0:
```python
import jax
import jax.numpy as jnp
from jax import lax
from jax.sharding import PartitionSpec as P


def crediting(totals):
    return 0.01 + jax.nn.softplus(20.0 * (totals[0] / totals[1] - 1.05)) / 20.0


def local(
    shocks,
    loadings,
    sec_drift,
    holdings,
    fund_of,
    product_type,
    term_years,
    asset_start,
    liab_start,
    base_lapse,
    guarantee,
    lapse_draw,
):
    highest = lax.Precision.HIGHEST
    num_years = shocks.shape[0]
    num_paths = shocks.shape[2]
    num_funds = holdings.shape[1]
    sec_ret = (
        0.25 * jnp.tanh(jnp.einsum("sk,ykp->ysp", loadings, shocks, precision=highest))
        + sec_drift[None, :, None]
    )
    partial_funds = jnp.einsum("sf,ysp->yfp", holdings, sec_ret, precision=highest)
    fund_ret = lax.psum(partial_funds, "pol")
    member = (fund_of[:, 0][:, None] == jnp.arange(num_funds, dtype=jnp.int32)[None, :]).astype(
        jnp.float32
    )
    type_hot = (
        product_type[:, None] == jnp.arange(base_lapse.shape[0], dtype=jnp.int32)[None, :]
    ).astype(jnp.float32)
    guaranteed = jnp.sum(type_hot * guarantee[None, :], axis=1)
    base_rate = jnp.sum(type_hot * base_lapse[None, :], axis=1)
    count = asset_start.shape[0]
    assets = jnp.broadcast_to(asset_start[:, None], (count, num_paths))
    liability = jnp.broadcast_to(liab_start[:, None], (count, num_paths))
    owned_paths = num_paths // lax.axis_size("pol")
    first_path = lax.axis_index("pol") * owned_paths
    collected = []
    for year in range(num_years):
        year_ret = fund_ret[year]
        in_force = (term_years > year).astype(jnp.float32)[:, None]
        growth = jnp.dot(member, year_ret, precision=highest)
        assets = assets * (1.0 + in_force * growth)
        fund_sums = jnp.stack(
            [
                jnp.dot(member.T, in_force * assets, precision=highest),
                jnp.dot(member.T, liability, precision=highest),
            ]
        )
        totals = lax.psum(fund_sums, "pol")
        declared = crediting(totals)
        own_rates = lax.dynamic_slice_in_dim(declared, first_path, owned_paths, 1)
        collected.append(own_rates)
        credit = jnp.maximum(jnp.dot(member, declared, precision=highest), guaranteed[:, None])
        lapse_rate = jnp.minimum(
            base_rate[:, None]
            * (0.5 + lapse_draw[:, year, :].astype(jnp.float32))
            * jnp.exp(5.0 * (growth - credit)),
            0.5,
        )
        liability = liability * (1.0 + in_force * credit) * (1.0 - in_force * lapse_rate)
        assets = assets * (1.0 - in_force * lapse_rate)
    return (assets, liability, jnp.stack(collected))


def solution(mesh):
    in_specs = (
        P("grp", None, None),
        P("pol", None),
        P("pol"),
        P("pol", None),
        P("pol", None),
        P("pol"),
        P("pol"),
        P("pol"),
        P("pol"),
        P(),
        P(),
        P("pol", "grp", None),
    )
    out_specs = (P("pol", "grp"), P("pol", "grp"), P("grp", None, "pol"))
    return jax.shard_map(local, mesh=mesh, in_specs=in_specs, out_specs=out_specs, check_vma=False)
```

profile of v0, /device:TPU:0, one launch (start us, length us, event | category | flops | bytes accessed | tf_op | source)
XLA Modules:
  0.0 433.8 jit_solution(17481085283756002193)
XLA Ops:
  7.2 0.0 copy-start
  7.2 0.0 copy-start.12
  7.2 0.0 all-reduce.5.cloned.1.call-start
  7.2 1.3 copy-done
  8.6 1.8 fusion.20
  10.4 0.0 copy-done.12
  10.4 0.0 copy-start.11
  10.4 0.0 copy-start.17
  10.4 0.0 copy-start.14
  10.4 3.8 convolution_bitcast_fusion
  14.2 0.0 all-reduce.5.cloned.1.call-update
  14.2 0.0 all-reduce.7.cloned.1.call-start
  14.3 0.0 copy-done.11
  14.3 1.6 convolution_bitcast_fusion.3
  15.9 0.0 copy-done.14
  15.9 97.1 %all-reduce.5.cloned.1.call-done = f32[3,128,1024]{1,2,0:T(8,128)} async-done(((f32[3,128,1024]{1,2,0:T(8,128)}), f32[3,128,1024]{1,2,0:T(8,128)}) %all-reduce.5.cloned.1.call-update) | async-done | bytes 1572880 | tf_op jit(solution)/shard_map/psum | solution.py:34
  113.0 2.1 fusion.53
  115.1 0.0 copy-start.7
  115.1 0.0 copy-start.10
  115.1 1.3 copy-done.7
  116.4 0.0 copy-done.18
  116.4 1.3 fusion.27
  117.7 0.0 copy-done.10
  117.7 0.0 copy-start.13
  117.7 0.0 copy-start.15
  117.7 0.0 copy-start.16
  117.7 1.0 pad_maximum_fusion
  118.8 0.0 all-reduce.7.cloned.1.call-update
  118.8 0.0 all-reduce.9.cloned.1.call-start
  118.9 0.1 select_reduce_fusion.1
  119.0 0.6 copy-done.8
  119.5 2.3 fusion.49
  121.9 89.7 %all-reduce.7.cloned.1.call-done = f32[2,128,1024]{2,1,0:T(8,128)} async-done(((f32[2,128,1024]{2,1,0:T(8,128)}), f32[2,128,1024]{2,1,0:T(8,128)}) %all-reduce.7.cloned.1.call-update) | async-done | bytes 1048592 | tf_op jit(solution)/shard_map/psum | solution.py:60
  211.5 1.6 fusion.37
  213.1 0.0 copy-start.9
  213.1 4.7 %multiply_multiply_fusion.2 = (f32[512,1024]{1,0:T(8,128)S(1)}, f32[512,1024]{1,0:T(8,128)S(1)}) fusion(f32[512,1024]{1,0:T(8,128)} %copy-done.7, f32[512]{0:T(512)S(1)} %get-tuple-element.4, f32[512]{0:T(512)S(1)} %get-tuple-element.3, f32[512]{0:T(512)S(1)} %get-tuple-element.11, f32[512]{0:T(512)S(1)} %copy-done.17, bf16[512,3,1024]{2,0,1:T(8,128)(2,1)} %param.23, ...), kind=kOutput, calls=%fused_computation.20 | convolution fusion | flops 816381952 | bytes 9975808 | tf_op jit(solution)/shard_map/dot_general | solution.py:64
  217.9 0.0 copy-start.6
  217.9 1.1 fusion.21
  219.0 1.0 convolution_bitcast_fusion.2
  220.0 1.1 pad_maximum_fusion.1
  221.0 0.0 all-reduce.9.cloned.1.call-update
  221.1 0.2 all-reduce.11.cloned.1.call-start
  221.3 2.3 fusion.45
  223.6 90.4 %all-reduce.9.cloned.1.call-done = f32[2,128,1024]{2,1,0:T(8,128)} async-done(((f32[2,128,1024]{2,1,0:T(8,128)}), f32[2,128,1024]{2,1,0:T(8,128)}) %all-reduce.9.cloned.1.call-update) | async-done | bytes 1048592 | tf_op jit(solution)/shard_map/psum | solution.py:60
  314.1 1.6 fusion.39
  315.7 4.2 multiply_multiply_fusion.1
  319.9 0.0 copy-start.4
  319.9 0.0 copy-start.5
  319.9 1.0 convolution_bitcast_fusion.1
  320.9 2.1 copy-done.2
  323.0 1.3 fusion.24
  324.4 0.0 copy-done.4
  324.4 0.0 copy-done.5
  324.4 1.1 pad_maximum_fusion.2
  325.5 0.0 all-reduce.11.cloned.1.call-update
  325.5 0.9 constant_dynamic-slice_fusion.2
  326.4 0.1 copy.18
  326.5 92.0 %all-reduce.11.cloned.1.call-done = f32[2,128,1024]{2,1,0:T(8,128)} async-done(((f32[2,128,1024]{2,1,0:T(8,128)}), f32[2,128,1024]{2,1,0:T(8,128)}) %all-reduce.11.cloned.1.call-update) | async-done | bytes 1048592 | tf_op jit(solution)/shard_map/psum | solution.py:60
  418.4 1.6 fusion.41
  420.0 0.1 constant_dynamic-slice_fusion
  420.1 6.3 %multiply_multiply_fusion = (f32[512,1024]{1,0:T(8,128)}, f32[512,1024]{1,0:T(8,128)}) fusion(f32[512,1024]{1,0:T(8,128)} %copy-done.5, f32[512]{0:T(512)S(1)} %get-tuple-element.12, f32[512]{0:T(512)S(1)} %get-tuple-element.4, f32[512,1024]{1,0:T(8,128)} %fusion.45, bf16[512,3,1024]{2,0,1:T(8,128)(2,1)} %param.23, f32[512]{0:T(512)S(1)} %get-tuple-element.3, ...), kind=kOutput, calls=%fused_computation.15 | convolution fusion | flops 815333376 | bytes 14163968 | tf_op jit(solution)/shard_map/dot_general | solution.py:64
  426.5 0.1 copy.19
  426.5 0.1 copy.20
  426.6 0.7 pad_maximum_fusion.3
  (14 shorter events, 0.0 us)
Async XLA Ops:
  7.2 1.4 copy-start
  7.2 3.2 copy-start.12
  7.2 105.8 %all-reduce.5.cloned.1.call-start = ((), (), s32[]{:S(2)}) async-start(), calls=%async_computation | async-start | bytes 3145728 | tf_op jit(solution)/shard_map/psum | solution.py:34
  10.4 3.9 copy-start.11
  10.4 3.9 copy-start.17
  10.4 5.5 %copy-start.14 = (s32[512]{0:T(512)S(1)}, s32[512]{0:T(512)}, u32[]{:S(2)}) copy-start(s32[512]{0:T(512)} %param.18) | copy-start | bytes 6148
  14.2 102.2 %copy-start.18 = (f32[512]{0:T(512)S(1)}, f32[512]{0:T(512)}, u32[]{:S(2)}) copy-start(f32[512]{0:T(512)} %param.19) | copy-start | bytes 6148
  14.2 197.3 %all-reduce.7.cloned.1.call-start = ((), (), s32[]{:S(2)}) async-start(), calls=%async_computation.1 | async-start | bytes 2097152 | tf_op jit(solution)/shard_map/psum | solution.py:60
  115.1 1.3 copy-start.7
  115.1 2.6 copy-start.10
  117.7 1.2 copy-start.13
  117.7 1.2 copy-start.15
  117.7 1.1 copy-start.16
  117.7 1.8 copy-start.8
  118.8 195.3 %all-reduce.9.cloned.1.call-start = ((), (), s32[]{:S(2)}) async-start(), calls=%async_computation.2 | async-start | bytes 2097152 | tf_op jit(solution)/shard_map/psum | solution.py:60
  213.1 4.8 %copy-start.9 = (f32[128,1024]{1,0:T(8,128)}, f32[128,1024]{1,0:T(8,128)S(1)}, u32[]{:S(2)}) copy-start(f32[128,1024]{1,0:T(8,128)S(1)} %fusion.37) | copy-start | bytes 1572868
  217.9 2.1 copy-start.1
  217.9 2.1 copy-start.6
  221.1 197.4 %all-reduce.11.cloned.1.call-start = ((), (), s32[]{:S(2)}) async-start(), calls=%async_computation.3 | async-start | bytes 2097152 | tf_op jit(solution)/shard_map/psum | solution.py:60
  315.7 5.2 %copy-start.3 = (f32[512,1024]{1,0:T(8,128)S(1)}, f32[512,1024]{1,0:T(8,128)}, u32[]{:S(2)}) copy-start(f32[512,1024]{1,0:T(8,128)} %fusion.45) | copy-start | bytes 6291460
  319.9 4.5 %copy-start.4 = (f32[512,1024]{1,0:T(8,128)}, f32[512,1024]{1,0:T(8,128)S(1)}, u32[]{:S(2)}) copy-start(f32[512,1024]{1,0:T(8,128)S(1)} %get-tuple-element.6) | copy-start | bytes 6291460
  319.9 4.5 %copy-start.5 = (f32[512,1024]{1,0:T(8,128)}, f32[512,1024]{1,0:T(8,128)S(1)}, u32[]{:S(2)}) copy-start(f32[512,1024]{1,0:T(8,128)S(1)} %get-tuple-element.5) | copy-start | bytes 6291460
  319.9 3.1 copy-start.2
Sparse Core Ops, SparseCore 0:
  14.4 98.6 all-reduce.4
  118.9 92.5 all-reduce.6
  221.2 92.8 all-reduce.8
  325.6 92.7 all-reduce.10
where the time goes:
time: 434 us
  waiting for transfers between devices  369 us (85%)
  matrix products  34.8 us (8%)
  between operations  14.1 us (3%)
  other arithmetic  8.72 us (2%)
  local copies, waits for them, and re-layouts  6.66 us (2%)
    psum x3, waiting for transfers between devices, local(): totals = lax.psum(fund_sums, 'pol')  272 us
    psum x1, waiting for transfers between devices, local(): fund_ret = lax.psum(partial_funds, 'pol')  97.1 us
    dot_general x3, matrix products, local(): jnp.dot(member, declared, precision=highest)  15.3 us
  transfers between devices with their start and end apart: 4, of which 4 were waited for; matrix products, arithmetic and copies ran while one was open for 2% of the time, Pallas kernels for 0%

commit v1 on v0

v1 whole, which is shorter than its diff:
```python
import functools

import jax
import jax.numpy as jnp
from jax import lax
from jax.experimental import pallas as pl
from jax.experimental.pallas import tpu as pltpu
from jax.sharding import PartitionSpec as P

MESH = pl.DeviceIdType.MESH
HIGHEST = lax.Precision.HIGHEST


def crediting(ra, rl):
    x = 20.0 * (ra / rl - 1.05)
    return 0.01 + (jnp.maximum(x, 0.0) + jnp.log1p(jnp.exp(-jnp.abs(x)))) / 20.0


def place():
    me = lax.axis_index("pol")
    chip, core = me // 2, me % 2
    return chip, core, chip * 2 + 1 - core


def greet(chips, chip, core, partner):
    barrier = pltpu.get_barrier_semaphore()
    pl.semaphore_signal(barrier, inc=1, device_id={"pol": partner}, device_id_type=MESH)
    for t in range(1, chips):
        other = lax.rem(chip + t, chips) * 2 + core
        pl.semaphore_signal(barrier, inc=1, device_id={"pol": other}, device_id_type=MESH)
    pl.semaphore_wait(barrier, chips)


def remote(src, dst, send, recv, device):
    return pltpu.make_async_remote_copy(
        src_ref=src,
        dst_ref=dst,
        send_sem=send,
        recv_sem=recv,
        device_id={"pol": device},
        device_id_type=MESH,
    )


def spread(chips, own_ref, all_ref, chip_send, chip_recv, core_send, core_recv):
    chip, core, partner = place()
    out = []
    for t in range(1, chips):
        device = lax.rem(chip + t, chips) * 2 + core
        copy = remote(own_ref, all_ref.at[chip, core], chip_send.at[t], chip_recv.at[t], device)
        copy.start()
        out.append(copy)
    first = remote(own_ref, all_ref.at[chip, core], core_send.at[0], core_recv.at[0], partner)
    first.start()
    all_ref[chip, core] = own_ref[...]
    forwards = [first]
    for t in range(1, chips):
        source = lax.rem(chip + chips - t, chips)
        slot = all_ref.at[source, core]
        out[t - 1].wait_recv()
        forward = remote(slot, slot, core_send.at[t], core_recv.at[t], partner)
        forward.start()
        forwards.append(forward)
    for copy in forwards:
        copy.wait_recv()
    for copy in out + forwards:
        copy.wait_send()


def gather_kernel(chips, own_ref, all_ref, chip_send, chip_recv, core_send, core_recv):
    greet(chips, *place())
    spread(chips, own_ref, all_ref, chip_send, chip_recv, core_send, core_recv)


def gather(own, chips):
    return pl.pallas_call(
        functools.partial(gather_kernel, chips),
        out_shape=jax.ShapeDtypeStruct((chips, 2) + own.shape, own.dtype),
        in_specs=[pl.BlockSpec(memory_space=pltpu.VMEM)],
        out_specs=pl.BlockSpec(memory_space=pltpu.VMEM),
        scratch_shapes=[pltpu.SemaphoreType.DMA((chips,))] * 4,
        compiler_params=pltpu.CompilerParams(collective_id=0, has_side_effects=True),
        name="gather",
    )(own)


def exchange_kernel(
    chips, sums, rates, theirs, mine, arrived, own, s1, r1, s2, r2, s3, r3, s4, r4
):
    chip, core, partner = place()
    greet(chips, chip, core, partner)
    order = list(range(1, chips)) + [0]
    across = {}
    for t in order:
        j = lax.rem(chip + t, chips)
        across[t] = remote(
            sums.at[:, j, 1 - core], theirs.at[j], s1.at[t], r1.at[t], partner
        )
        across[t].start()
    out = []
    for t in range(1, chips):
        j = lax.rem(chip + t, chips)
        across[t].wait_recv()
        mine[t] = sums[:, j, core] + theirs[j]
        copy = remote(mine.at[t], arrived.at[t], s2.at[t], r2.at[t], j * 2 + core)
        copy.start()
        out.append(copy)
    across[0].wait_recv()
    total = sums[:, chip, core] + theirs[chip]
    for t in range(1, chips):
        out[t - 1].wait_recv()
        total = total + arrived[t]
    own[...] = crediting(total[0], total[1])
    spread(chips, own, rates, s3, r3, s4, r4)
    for copy in list(across.values()) + out:
        copy.wait_send()


def exchange(sums, chips):
    rows, paths = sums.shape[3:]
    part = pltpu.VMEM((chips, 2, rows, paths), jnp.float32)
    return pl.pallas_call(
        functools.partial(exchange_kernel, chips),
        out_shape=jax.ShapeDtypeStruct((chips, 2, rows, paths), jnp.float32),
        in_specs=[pl.BlockSpec(memory_space=pltpu.VMEM)],
        out_specs=pl.BlockSpec(memory_space=pltpu.VMEM),
        scratch_shapes=[part, part, part, pltpu.VMEM((rows, paths), jnp.float32)]
        + [pltpu.SemaphoreType.DMA((chips,))] * 8,
        compiler_params=pltpu.CompilerParams(collective_id=1, has_side_effects=True),
        name="exchange",
    )(sums)


def split(x):
    high = x.astype(jnp.bfloat16)
    return high, (x - high.astype(jnp.float32)).astype(jnp.bfloat16)


def dot(a, b):
    return jnp.dot(a, b, preferred_element_type=jnp.float32)


def returns_kernel(secs, every, shocks, fund_ret, first, loads, holds, cols):
    chunk = pl.program_id(1)
    last = pl.num_programs(1) - 1
    group, _, funds = every.shape
    depth = group * secs

    @pl.when(pl.program_id(0) == 0)
    def _():
        high, low = split(every[:, :secs].reshape(depth, funds))
        loads[chunk] = jnp.concatenate([high, low], axis=1)
        high, low = split(every[:, secs : 2 * secs].reshape(depth, funds).T)
        holds[chunk] = jnp.concatenate([high, low], axis=0)

    extras = jnp.sum(every[:, 2 * secs :], axis=0)
    columns = jnp.concatenate([extras, jnp.zeros((funds - 8, funds), jnp.float32)], axis=0).T

    @pl.when(chunk == 0)
    def _():
        cols[...] = columns

    @pl.when(chunk > 0)
    def _():
        cols[...] += columns

    for year in range(shocks.shape[0]):
        high, low = split(shocks[year])
        exposure = dot(loads[chunk], jnp.concatenate([high, high], axis=0)) + dot(
            loads[chunk, :, :funds], low
        )
        high, low = split(0.25 * jnp.tanh(exposure))
        both = dot(holds[chunk], high)
        term = both[:funds] + both[funds:] + dot(holds[chunk, :funds], low)

        @pl.when(chunk == 0)
        def _():
            fund_ret[year] = term

        @pl.when(chunk > 0)
        def _():
            fund_ret[year] += term

        @pl.when(chunk == last)
        def _():
            fund_ret[year] += cols[:, 0:1]

    @pl.when(chunk == last)
    def _():
        first[...] = crediting(cols[:, 1:2] * (1.0 + fund_ret[0]), cols[:, 2:3])


def returns(every, shocks, secs):
    size, height, funds = every.shape
    years, factors, paths = shocks.shape
    group = min(size, 16)
    block = min(paths, 256)
    chunks = size // group
    depth = group * secs
    return pl.pallas_call(
        functools.partial(returns_kernel, secs),
        grid=(paths // block, chunks),
        out_shape=(
            jax.ShapeDtypeStruct((years, funds, paths), jnp.float32),
            jax.ShapeDtypeStruct((funds, paths), jnp.float32),
        ),
        in_specs=[
            pl.BlockSpec((group, height, funds), lambda p, c: (c, 0, 0)),
            pl.BlockSpec((years, factors, block), lambda p, c: (0, 0, p)),
        ],
        out_specs=(
            pl.BlockSpec((years, funds, block), lambda p, c: (0, 0, p)),
            pl.BlockSpec((funds, block), lambda p, c: (0, p)),
        ),
        scratch_shapes=[
            pltpu.VMEM((chunks, depth, 2 * factors), jnp.bfloat16),
            pltpu.VMEM((chunks, 2 * funds, depth), jnp.bfloat16),
            pltpu.VMEM((funds, funds), jnp.float32),
        ],
        name="returns",
    )(every, shocks)


def local(
    shocks,
    loadings,
    sec_drift,
    holdings,
    fund_of,
    product_type,
    term_years,
    asset_start,
    liab_start,
    base_lapse,
    guarantee,
    lapse_draw,
):
    num_years, num_factors, num_paths = shocks.shape
    secs, num_funds = holdings.shape
    size = lax.axis_size("pol")
    chips = size // 2
    rows = num_funds // size
    count = asset_start.shape[0]
    member = (fund_of[:, 0][:, None] == jnp.arange(num_funds, dtype=jnp.int32)[None, :]).astype(
        jnp.float32
    )
    first_force = (term_years > 0).astype(jnp.float32)
    extras = jnp.stack(
        [
            jnp.sum(holdings * sec_drift[:, None], axis=0),
            jnp.sum(member * (first_force * asset_start)[:, None], axis=0),
            jnp.sum(member * liab_start[:, None], axis=0),
        ]
    )
    extras = jnp.pad(extras, ((0, 5), (0, 0)))
    packed = jnp.concatenate([loadings, holdings, extras], axis=0)
    everyone = gather(packed, chips).reshape(size, 2 * secs + 8, num_funds)
    fund_ret, first_rates = returns(everyone, shocks, secs)

    type_hot = (
        product_type[:, None] == jnp.arange(base_lapse.shape[0], dtype=jnp.int32)[None, :]
    ).astype(jnp.float32)
    guaranteed = jnp.sum(type_hot * guarantee[None, :], axis=1)
    base_rate = jnp.sum(type_hot * base_lapse[None, :], axis=1)
    assets = jnp.broadcast_to(asset_start[:, None], (count, num_paths))
    liability = jnp.broadcast_to(liab_start[:, None], (count, num_paths))
    owned_paths = num_paths // size
    first_path = lax.axis_index("pol") * owned_paths
    collected = []
    for year in range(num_years):
        year_ret = fund_ret[year]
        in_force = (term_years > year).astype(jnp.float32)[:, None]
        growth = jnp.dot(member, year_ret, precision=HIGHEST)
        assets = assets * (1.0 + in_force * growth)
        if year == 0:
            declared = first_rates
        else:
            sums = jnp.stack(
                [
                    jnp.dot(member.T, in_force * assets, precision=HIGHEST),
                    jnp.dot(member.T, liability, precision=HIGHEST),
                ]
            )
            declared = exchange(sums.reshape(2, chips, 2, rows, num_paths), chips).reshape(
                num_funds, num_paths
            )
        own_rates = lax.dynamic_slice_in_dim(declared, first_path, owned_paths, 1)
        collected.append(own_rates)
        credit = jnp.maximum(jnp.dot(member, declared, precision=HIGHEST), guaranteed[:, None])
        lapse_rate = jnp.minimum(
            base_rate[:, None]
            * (0.5 + lapse_draw[:, year, :].astype(jnp.float32))
            * jnp.exp(5.0 * (growth - credit)),
            0.5,
        )
        liability = liability * (1.0 + in_force * credit) * (1.0 - in_force * lapse_rate)
        assets = assets * (1.0 - in_force * lapse_rate)
    return (assets, liability, jnp.stack(collected))


def solution(mesh):
    in_specs = (
        P("grp", None, None),
        P("pol", None),
        P("pol"),
        P("pol", None),
        P("pol", None),
        P("pol"),
        P("pol"),
        P("pol"),
        P("pol"),
        P(),
        P(),
        P("pol", "grp", None),
    )
    out_specs = (P("pol", "grp"), P("pol", "grp"), P("grp", None, "pol"))
    return jax.shard_map(local, mesh=mesh, in_specs=in_specs, out_specs=out_specs, check_vma=False)
```

time: 434 us -> 128 us (0.29)
  waiting for transfers between devices: 369 us -> 0 us
  Pallas kernels: 0 us -> 90.5 us
  between operations: 14.1 us -> 0.93 us
  matrix products: 34.8 us -> 27.1 us
  local copies, waits for them, and re-layouts: 6.66 us -> 1.35 us
    psum x4 -> x0, waiting for transfers between devices: 369 us -> none  [the longest x3 272 us: local(): totals = lax.psum(fund_sums, 'pol')]
    pallas_call x0 -> x4, Pallas kernels: none -> 90.5 us  [the longest x2 58.7 us: exchange(): pl.pallas_call(functools.partial(exchange_kernel, chips), out_shape=jax.S...]
    dot_general x14 -> x10, matrix products: 34.8 us -> 27.1 us  [the longest x3 15.7 us: local(): jnp.dot(member, declared, precision=HIGHEST)]
    unnamed x38 -> x24, local copies, waits for them, and re-layouts: 5.43 us -> 0.07 us
    add x3 -> x0, other arithmetic: 4.76 us -> none  [crediting(): return 0.01 + jax.nn.softplus(20.0 * (totals[0] / totals[1] - 1.05)) / 20.0]
  transfers between devices with their start and end apart: 4 -> 0, of which waited for: 4 -> 0; matrix products, arithmetic and copies ran while one was open for 2% -> 0% of each run, Pallas kernels for 0% -> 0%
where the time goes in v1:
time: 128 us; the launch traced here: 127 us
  Pallas kernels  90.5 us (71%)
  matrix products  27.1 us (21%)
  other arithmetic  7.5 us (6%)
  local copies, waits for them, and re-layouts  1.35 us (1%)
    pallas_call x2, Pallas kernels, exchange(): pl.pallas_call(functools.partial(exchange_kernel, chips), out_shape=jax.S...  58.7 us
    pallas_call x1, Pallas kernels, gather(): pl.pallas_call(functools.partial(gather_kernel, chips), out_shape=jax.Sha...  18.4 us
    dot_general x3, matrix products, local(): jnp.dot(member, declared, precision=HIGHEST)  15.7 us
    pallas_call x1, Pallas kernels, returns(): pl.pallas_call(functools.partial(returns_kernel, secs), grid=(paths // bl...  13.4 us
    dot_general x3, matrix products, local(): growth = jnp.dot(member, year_ret, precision=HIGHEST)  7.04 us

profile of v1, /device:TPU:0, one launch (start us, length us, event | category | flops | bytes accessed | tf_op | source)
XLA Modules:
  0.0 127.4 jit_solution(16481040494807113377)
XLA Ops:
  0.6 0.0 copy-start.5
  0.6 0.7 fusion.44
  1.3 0.7 broadcast_select_fusion
  2.0 1.0 select_reduce_fusion.1
  3.0 0.9 multiply_reduce_fusion
  3.9 1.4 %pad_maximum_fusion.3.own_ref = f32[136,128]{1,0:T(8,128)} fusion(f32[8,128]{1,0:T(8,128)S(1)} %select_maximum_fusion, f32[64,128]{1,0:T(8,128)} %param.15, f32[64,128]{1,0:T(8,128)} %param.13), kind=kLoop, calls=%fused_computation.56 | loop fusion | flops 34816 | bytes 139264 | tf_op jit(solution)/shard_map/concatenate | solution.py:256
  5.3 18.4 %gather.1 = f32[8,2,136,128]{3,2,1,0:T(8,128)} custom-call(f32[136,128]{1,0:T(8,128)} %pad_maximum_fusion.3.own_ref), custom_call_target="tpu_custom_call" | custom-call | tf_op jit(solution)/shard_map/gather/pallas_call | solution.py:76
  23.7 13.4 %returns.1 = (f32[3,128,1024]{2,1,0:T(8,128)}, f32[128,1024]{1,0:T(8,128)}) custom-call(f32[16,136,128]{2,1,0:T(8,128)} %bitcast.67, f32[3,128,1024]{2,1,0:T(8,128)} %shocks.1), custom_call_target="tpu_custom_call" | custom-call | tf_op jit(solution)/shard_map/returns/pallas_call | solution.py:200
  37.1 0.0 copy-done.5
  37.1 0.0 copy-start.7
  37.1 0.0 copy-start.10
  37.1 0.0 copy-start.11
  37.1 0.0 copy-start.6
  37.2 0.0 copy-start.8
  37.2 0.0 copy-start.9
  37.2 2.1 %fusion.20 = f32[512,1024]{1,0:T(8,128)S(1)} fusion(f32[3,128,1024]{2,1,0:T(8,128)} %get-tuple-element.5, s32[512]{0:T(512)S(1)} %bitcast.77), kind=kOutput, calls=%fused_computation.30 | convolution fusion | flops 805371904 | bytes 2623488 | tf_op jit(solution)/shard_map/dot_general | solution.py:273
  39.3 0.0 copy-start.3
  39.3 2.4 %fusion.22 = f32[512,1024]{1,0:T(8,128)S(1)} fusion(f32[3,128,1024]{2,1,0:T(8,128)} %get-tuple-element.5, s32[512]{0:T(512)S(1)} %bitcast.78), kind=kOutput, calls=%fused_computation.32 | convolution fusion | flops 805371904 | bytes 2623488 | tf_op jit(solution)/shard_map/dot_general | solution.py:273
  41.8 0.0 copy-done.7
  41.8 0.0 copy-done.10
  41.8 0.0 copy-done.11
  41.8 0.1 select_reduce_fusion.3
  41.9 0.0 copy-done.6
  41.9 0.0 copy-done.8
  41.9 0.0 copy-done.9
  41.9 3.9 %multiply_multiply_fusion.2 = (f32[512,1024]{1,0:T(8,128)S(1)}, f32[512,1024]{1,0:T(8,128)S(1)}) fusion(f32[512,1024]{1,0:T(8,128)S(1)} %fusion.22, f32[512]{0:T(512)S(1)} %copy-done.8, f32[512]{0:T(512)S(1)} %get-tuple-element.8, f32[512]{0:T(512)S(1)} %get-tuple-element.7, f32[512]{0:T(512)S(1)} %get-tuple-element.13, bf16[512,3,1024]{2,0,1:T(8,128)(2,1)} %param.23, ...), kind=kOutput, calls=%fused_computation.20 | convolution fusion | flops 816381952 | bytes 9975808 | tf_op jit(solution)/shard_map/dot_general | solution.py:289
  45.9 0.0 copy-done.3
  45.9 0.0 copy-start.4
  45.9 1.0 fusion.14
  46.9 1.0 fusion.30
  47.9 0.0 copy-done.4
  47.9 1.0 pad_maximum_fusion.sums
  49.0 33.1 %exchange.2 = f32[8,2,8,1024]{3,2,1,0:T(8,128)} custom-call(f32[2,8,2,8,1024]{4,3,2,1,0:T(8,128)} %pad_maximum_fusion.sums), custom_call_target="tpu_custom_call" | custom-call | tf_op jit(solution)/shard_map/exchange/pallas_call | solution.py:122
  82.1 5.0 %multiply_multiply_fusion.1 = (f32[512,1024]{1,0:T(8,128)S(1)}, f32[512,1024]{1,0:T(8,128)S(1)}) fusion(f32[512,1024]{1,0:T(8,128)} %copy-done.4, f32[512]{0:T(512)S(1)} %get-tuple-element.19, f32[512]{0:T(512)S(1)} %get-tuple-element.8, f32[512,1024]{1,0:T(8,128)} %copy-done.3, bf16[512,3,1024]{2,0,1:T(8,128)(2,1)} %param.23, ...), kind=kOutput, calls=%fused_computation.16 | convolution fusion | flops 812711936 | bytes 9969664 | tf_op jit(solution)/shard_map/dot_general | solution.py:289
  87.1 0.0 copy-start.1
  87.1 0.0 copy-start.2
  87.1 2.5 %fusion.18 = f32[512,1024]{1,0:T(8,128)S(1)} fusion(f32[3,128,1024]{2,1,0:T(8,128)} %get-tuple-element.5, s32[512]{0:T(512)S(1)} %bitcast.83), kind=kOutput, calls=%fused_computation.28 | convolution fusion | flops 805371904 | bytes 2623488 | tf_op jit(solution)/shard_map/dot_general | solution.py:273
  89.6 0.0 copy-start
  89.6 1.4 %fusion.12 = f32[128,1024]{1,0:T(8,128)S(1)} fusion(f32[512]{0:T(512)S(1)} %get-tuple-element.20, s32[512]{0:T(512)S(1)} %bitcast.84, f32[512,1024]{1,0:T(8,128)S(1)} %fusion.18, f32[512,1024]{1,0:T(8,128)S(1)} %get-tuple-element.18, f32[512,1024]{1,0:T(8,128)S(1)} %get-tuple-element.12), kind=kOutput, calls=%fused_computation.17 | convolution fusion | flops 807993344 | bytes 6819840 | tf_op jit(solution)/shard_map/dot_general | solution.py:280
  91.0 0.0 copy-done.1
  91.0 0.0 copy-done
  91.0 0.0 copy-done.2
  91.0 1.0 fusion.28
  92.0 1.1 pad_maximum_fusion.1.sums
  93.1 25.6 %exchange.3 = f32[8,2,8,1024]{3,2,1,0:T(8,128)} custom-call(f32[2,8,2,8,1024]{4,3,2,1,0:T(8,128)} %pad_maximum_fusion.1.sums), custom_call_target="tpu_custom_call" | custom-call | tf_op jit(solution)/shard_map/exchange/pallas_call | solution.py:122
  118.7 1.0 constant_dynamic-slice_fusion
  119.6 0.1 copy.21
  119.7 0.1 copy.22
  119.8 0.1 constant_dynamic-slice_fusion.2
  119.9 0.1 copy.20
  120.0 0.7 pad_maximum_fusion.2
  120.6 6.7 %multiply_multiply_fusion = (f32[512,1024]{1,0:T(8,128)}, f32[512,1024]{1,0:T(8,128)}) fusion(f32[512,1024]{1,0:T(8,128)} %copy-done.2, f32[512]{0:T(512)S(1)} %get-tuple-element.20, f32[512]{0:T(512)S(1)} %get-tuple-element.8, f32[512,1024]{1,0:T(8,128)} %copy-done, bf16[512,3,1024]{2,0,1:T(8,128)(2,1)} %param.23, f32[512]{0:T(512)S(1)} %get-tuple-element.7, ...), kind=kOutput, calls=%fused_computation.15 | convolution fusion | flops 815333376 | bytes 14163968 | tf_op jit(solution)/shard_map/dot_general | solution.py:289
  (1 shorter events, 0.0 us)
Async XLA Ops:
  0.6 36.5 %copy-start.5 = (s32[512,1]{0,1:T(1,128)S(1)}, s32[512,1]{0,1:T(1,128)}, u32[]{:S(2)}) copy-start(s32[512,1]{0,1:T(1,128)} %param.16) | copy-start | bytes 6148
  37.1 4.7 %copy-start.7 = (s32[512]{0:T(512)S(1)}, s32[512]{0:T(512)}, u32[]{:S(2)}) copy-start(s32[512]{0:T(512)} %param.17) | copy-start | bytes 6148
  37.1 4.7 %copy-start.10 = (f32[8]{0:T(128)S(1)}, f32[8]{0:T(128)}, u32[]{:S(2)}) copy-start(f32[8]{0:T(128)} %param.21) | copy-start | bytes 100
  37.1 4.7 %copy-start.11 = (f32[8]{0:T(128)S(1)}, f32[8]{0:T(128)}, u32[]{:S(2)}) copy-start(f32[8]{0:T(128)} %param.22) | copy-start | bytes 100
  37.1 4.8 %copy-start.6 = (f32[128,1024]{1,0:T(8,128)S(1)}, f32[128,1024]{1,0:T(8,128)}, u32[]{:S(2)}) copy-start(f32[128,1024]{1,0:T(8,128)} %get-tuple-element.6) | copy-start | bytes 1572868
  37.2 4.8 %copy-start.8 = (f32[512]{0:T(512)S(1)}, f32[512]{0:T(512)}, u32[]{:S(2)}) copy-start(f32[512]{0:T(512)} %param.20) | copy-start | bytes 6148
  37.2 4.8 %copy-start.9 = (f32[512]{0:T(512)S(1)}, f32[512]{0:T(512)}, u32[]{:S(2)}) copy-start(f32[512]{0:T(512)} %param.19) | copy-start | bytes 6148
  39.3 6.5 %copy-start.3 = (f32[512,1024]{1,0:T(8,128)}, f32[512,1024]{1,0:T(8,128)S(1)}, u32[]{:S(2)}) copy-start(f32[512,1024]{1,0:T(8,128)S(1)} %fusion.20) | copy-start | bytes 6291460
  45.9 2.0 %copy-start.4 = (f32[512,1024]{1,0:T(8,128)}, f32[512,1024]{1,0:T(8,128)S(1)}, u32[]{:S(2)}) copy-start(f32[512,1024]{1,0:T(8,128)S(1)} %get-tuple-element.17) | copy-start | bytes 6291460
  87.1 3.9 %copy-start.1 = (f32[512,1024]{1,0:T(8,128)}, f32[512,1024]{1,0:T(8,128)S(1)}, u32[]{:S(2)}) copy-start(f32[512,1024]{1,0:T(8,128)S(1)} %get-tuple-element.12) | copy-start | bytes 6291460
  87.1 3.9 %copy-start.2 = (f32[512,1024]{1,0:T(8,128)}, f32[512,1024]{1,0:T(8,128)S(1)}, u32[]{:S(2)}) copy-start(f32[512,1024]{1,0:T(8,128)S(1)} %get-tuple-element.11) | copy-start | bytes 6291460
  89.6 1.4 %copy-start = (f32[512,1024]{1,0:T(8,128)}, f32[512,1024]{1,0:T(8,128)S(1)}, u32[]{:S(2)}) copy-start(f32[512,1024]{1,0:T(8,128)S(1)} %fusion.18) | copy-start | bytes 6291460

commit v2 on v0

v2 whole, which is shorter than its diff:
```python
import functools

import jax
import jax.numpy as jnp
from jax import lax
from jax.experimental import pallas as pl
from jax.experimental.pallas import tpu as pltpu
from jax.sharding import PartitionSpec as P

MESH = pl.DeviceIdType.MESH
HIGHEST = lax.Precision.HIGHEST
PARTS = 2
LANES = 256
ROWS = 256


def crediting(ra, rl):
    x = 20.0 * (ra / rl - 1.05)
    return 0.01 + (jnp.maximum(x, 0.0) + jnp.log1p(jnp.exp(-jnp.abs(x)))) / 20.0


def split(x):
    high = x.astype(jnp.bfloat16)
    return high, (x - high.astype(jnp.float32)).astype(jnp.bfloat16)


def stacked(x):
    return jnp.concatenate(split(x), axis=0)


def dot(a, b):
    return jnp.dot(a, b, preferred_element_type=jnp.float32)


class Place:
    def __init__(self, depth):
        me = lax.axis_index("pol")
        self.depth = depth
        self.core = lax.rem(me, 2)
        self.x = lax.rem(me // 2, 2)
        self.z = me // 4

    def device(self, z, x, core):
        return (z * 2 + x) * 2 + core

    def ahead(self, t):
        return lax.rem(self.z + t, self.depth)

    def behind(self, t):
        return lax.rem(self.z + self.depth - t, self.depth)

    def to_core(self):
        return self.device(self.z, self.x, 1 - self.core)

    def to_x(self):
        return self.device(self.z, 1 - self.x, self.core)

    def to_z(self, t):
        return self.device(self.ahead(t), self.x, self.core)

    def greet(self):
        barrier = pltpu.get_barrier_semaphore()
        others = [self.to_core(), self.to_x()] + [self.to_z(t) for t in range(1, self.depth)]
        for other in others:
            pl.semaphore_signal(barrier, inc=1, device_id={"pol": other}, device_id_type=MESH)
        pl.semaphore_wait(barrier, len(others))


def send(src, dst, sems, at, device):
    copy = pltpu.make_async_remote_copy(
        src_ref=src,
        dst_ref=dst,
        send_sem=sems.at[0, at],
        recv_sem=sems.at[1, at],
        device_id={"pol": device},
        device_id_type=MESH,
    )
    copy.start()
    return copy


class Spread:
    def __init__(self, place, own, every, sems):
        self.p, self.own, self.every, self.sems = place, own, every, sems

    def start(self):
        p, n = self.p, self.p.depth
        slot = self.every.at[p.z, p.x, p.core]
        self.along = [send(self.own, slot, self.sems, t, p.to_z(t)) for t in range(1, n)]
        self.across = [send(self.own, slot, self.sems, n, p.to_x())]
        self.pair = [send(self.own, slot, self.sems, 2 * n, p.to_core())]
        self.every[p.z, p.x, p.core] = self.own[...]

    def relay_z(self):
        p, n = self.p, self.p.depth
        for t in range(1, n):
            self.along[t - 1].wait_recv()
            slot = self.every.at[p.behind(t), p.x, p.core]
            self.across.append(send(slot, slot, self.sems, n + t, p.to_x()))
            self.pair.append(send(slot, slot, self.sems, 2 * n + t, p.to_core()))

    def relay_x(self):
        p, n = self.p, self.p.depth
        for t in range(n):
            self.across[t].wait_recv()
            slot = self.every.at[p.behind(t), 1 - p.x, p.core]
            self.pair.append(send(slot, slot, self.sems, 3 * n + t, p.to_core()))

    def finish(self):
        for copy in self.pair:
            copy.wait_recv()
        for copy in self.along + self.across + self.pair:
            copy.wait_send()


class Totals:
    def __init__(self, place, sums, pair_in, x_out, x_in, z_out, z_in, sems):
        self.p, self.sums, self.pair_in, self.sems = place, sums, pair_in, sems
        self.x_out, self.x_in, self.z_out, self.z_in = x_out, x_in, z_out, z_in
        self.order = list(range(1, place.depth)) + [0]

    def start(self):
        p, n = self.p, self.p.depth
        self.pair = {}
        for x, base in ((1 - p.x, 0), (p.x, n)):
            for t in self.order:
                z = p.ahead(t)
                self.pair[base + t] = send(
                    self.sums.at[:, z, x, 1 - p.core],
                    self.pair_in.at[z, x],
                    self.sems,
                    base + t,
                    p.to_core(),
                )

    def add_x(self):
        p, n = self.p, self.p.depth
        self.across = {}
        for t in self.order:
            z = p.ahead(t)
            self.pair[t].wait_recv()
            self.x_out[t] = self.sums[:, z, 1 - p.x, p.core] + self.pair_in[z, 1 - p.x]
            self.across[t] = send(
                self.x_out.at[t], self.x_in.at[t], self.sems, 2 * n + t, p.to_x()
            )

    def chip_sum(self, t):
        p, n = self.p, self.p.depth
        z = p.ahead(t)
        self.pair[n + t].wait_recv()
        self.across[t].wait_recv()
        return self.sums[:, z, p.x, p.core] + self.pair_in[z, p.x] + self.x_in[t]

    def add_z(self):
        p, n = self.p, self.p.depth
        self.along = {}
        for t in range(1, n):
            self.z_out[t] = self.chip_sum(t)
            self.along[t] = send(
                self.z_out.at[t], self.z_in.at[t], self.sems, 3 * n + t, p.to_z(t)
            )

    def finish(self):
        total = self.chip_sum(0)
        for t in range(1, self.p.depth):
            self.along[t].wait_recv()
            total = total + self.z_in[t]
        return total

    def settle(self):
        for group in (self.pair, self.across, self.along):
            for copy in group.values():
                copy.wait_send()


def year_step(member, hot, force, base, floor, growth_of, credit_of, draw, assets, liability):
    growth = dot(member, growth_of)
    credit = jnp.maximum(dot(member, credit_of), floor)
    assets = assets * (1.0 + force * growth)
    lapse = force * jnp.minimum(
        base * (0.5 + draw.astype(jnp.float32)) * jnp.exp(5.0 * (growth - credit)), 0.5
    )
    stay = 1.0 - lapse
    return assets * stay, liability * (1.0 + force * credit) * stay


def main_kernel(
    base_lapse,
    guarantee,
    fund_row,
    type_row,
    term_row,
    asset_row,
    liab_row,
    drift_row,
    loadings,
    holdings,
    shocks_hbm,
    draws_hbm,
    assets,
    liability,
    fund_ret,
    rates,
    member,
    columns,
    shocks,
    draws,
    packed,
    every,
    loads,
    holds,
    hots,
    extra_columns,
    sums,
    pair_in,
    x_out,
    x_in,
    z_out,
    z_in,
    own,
    local_sems,
    gather_sems,
    total_sems,
    spread_sems,
):
    depth = every.shape[0]
    secs, funds = holdings.shape
    count = fund_row.shape[1]
    years = shocks.shape[0]
    width = assets.shape[2]
    groups, group_secs, _ = loads.shape
    place = Place(depth)

    fetch_shocks = pltpu.make_async_copy(shocks_hbm, shocks, local_sems.at[0])
    fetch_draws = pltpu.make_async_copy(
        draws_hbm.at[pl.ds(0, years - 1)], draws, local_sems.at[1]
    )
    fetch_shocks.start()
    fetch_draws.start()

    fund_id = lax.broadcasted_iota(jnp.int32, (funds, count), 0)
    hot = fund_row[...] == fund_id
    hot_rows = hot.astype(jnp.float32)
    floor = jnp.zeros((1, count), jnp.float32)
    base = jnp.zeros((1, count), jnp.float32)
    for kind in range(guarantee.shape[0]):
        same = type_row[...] == kind
        floor = jnp.where(same, guarantee[kind], floor)
        base = jnp.where(same, base_lapse[kind], base)
    in_force = [(term_row[...] > year).astype(jnp.float32) for year in range(years)]
    row = lax.broadcasted_iota(jnp.int32, (funds, count), 0)
    table = jnp.zeros((funds, count), jnp.float32)
    for at, values in enumerate([floor, base, asset_row[...], liab_row[...]] + in_force):
        table = jnp.where(row == at, values, table)
    columns[...] = table.T
    starts = jnp.concatenate(
        [in_force[0] * asset_row[...], liab_row[...], jnp.zeros((6, count), jnp.float32)], axis=0
    )
    member_f32 = hot_rows.T
    start_sums = jnp.dot(starts, member_f32, precision=HIGHEST)
    drifts = jnp.broadcast_to(drift_row[...], (8, secs))
    drift_sums = jnp.dot(drifts, holdings[...], precision=HIGHEST)
    packed[:secs] = loadings[...]
    packed[secs : 2 * secs] = holdings[...]
    packed[2 * secs : 2 * secs + 8] = drift_sums
    packed[2 * secs + 8 :] = start_sums

    place.greet()
    gather = Spread(place, packed, every, gather_sems)
    gather.start()
    narrow = member_f32.astype(jnp.bfloat16)
    member[...] = jnp.concatenate([narrow, narrow], axis=1)
    hots[0] = hot_rows.astype(jnp.bfloat16)
    for year in range(1, years):
        hots[year] = jnp.where(in_force[year] > 0.0, hot_rows, 0.0).astype(jnp.bfloat16)
    gather.relay_z()
    gather.relay_x()
    gather.finish()
    fetch_shocks.wait()
    fetch_draws.wait()

    per = group_secs // secs
    flat = every.shape[0] * 4
    extra = jnp.zeros((16, funds), jnp.float32)
    for device in range(flat):
        extra += every[device // 4, (device // 2) % 2, device % 2, 2 * secs :]
    extra_columns[...] = jnp.concatenate(
        [extra, jnp.zeros((funds - 16, funds), jnp.float32)], axis=0
    ).T

    def prepare(at, _):
        block = every[at]
        high, low = split(block[:, :, :secs].reshape(group_secs, funds))
        loads[at] = jnp.concatenate([high, low], axis=1)
        high, low = split(block[:, :, secs : 2 * secs].reshape(group_secs, funds).T)
        holds[at] = jnp.concatenate([high, low], axis=0)
        return 0

    lax.fori_loop(0, groups, prepare, 0)

    def returns(part, year):
        high, low = split(shocks[year, :, part * width : (part + 1) * width])
        twice = jnp.concatenate([high, high], axis=0)

        def step(at, total):
            exposure = dot(loads[at], twice) + dot(loads[at, :, :funds], low)
            t_high, t_low = split(0.25 * jnp.tanh(exposure))
            both = dot(holds[at], t_high)
            return total + both[:funds] + both[funds:] + dot(holds[at, :funds], t_low)

        total = lax.fori_loop(0, groups, step, jnp.zeros((funds, width), jnp.float32))
        fund_ret[year, part] = total + extra_columns[:, 0:1]

    def first_rates(part):
        declared = crediting(
            extra_columns[:, 8:9] * (1.0 + fund_ret[0, part]), extra_columns[:, 9:10]
        )
        rates[0, part] = declared.reshape(rates.shape[2:])

    def advance(part, year):
        def step(block, _):
            lanes = pl.ds(pl.multiple_of(block * LANES, LANES), LANES)
            growth_of = stacked(fund_ret[year, part, :, lanes])
            declared = rates[year, part, :, :, :, :, lanes].reshape(funds, LANES)
            credit_of = stacked(declared)
            asset_sum = jnp.zeros((funds, LANES), jnp.float32)
            liab_sum = jnp.zeros((funds, LANES), jnp.float32)
            for first in range(0, count, ROWS):
                rows = slice(first, first + ROWS)
                if year == 0:
                    held = jnp.broadcast_to(columns[rows, 2:3], (ROWS, LANES))
                    owed = jnp.broadcast_to(columns[rows, 3:4], (ROWS, LANES))
                else:
                    held = assets[part, rows, lanes]
                    owed = liability[part, rows, lanes]
                draw_at = pl.ds(pl.multiple_of(part * width + block * LANES, LANES), LANES)
                held, owed = year_step(
                    member[rows],
                    None,
                    columns[rows, 4 + year : 5 + year],
                    columns[rows, 1:2],
                    columns[rows, 0:1],
                    growth_of,
                    credit_of,
                    draws[year, rows, draw_at],
                    held,
                    owed,
                )
                assets[part, rows, lanes] = held
                liability[part, rows, lanes] = owed
                high, low = split(held)
                pick = hots[year + 1, :, rows]
                asset_sum += dot(pick, high) + dot(pick, low)
                high, low = split(owed)
                pick = hots[0, :, rows]
                liab_sum += dot(pick, high) + dot(pick, low)
            asset_sum = asset_sum * (1.0 + fund_ret[year + 1, part, :, lanes])
            shape = sums.shape[2:6] + (LANES,)
            sums[part, 0, :, :, :, :, lanes] = asset_sum.reshape(shape)
            sums[part, 1, :, :, :, :, lanes] = liab_sum.reshape(shape)
            return 0

        lax.fori_loop(0, width // LANES, step, 0)

    def totals(part):
        return Totals(
            place,
            sums.at[part],
            pair_in.at[part],
            x_out.at[part],
            x_in.at[part],
            z_out.at[part],
            z_in.at[part],
            total_sems.at[part],
        )

    def declare(total, year, part):
        summed = total.finish()
        own[part] = crediting(summed[0], summed[1])
        spread = Spread(place, own.at[part], rates.at[year, part], spread_sems.at[part])
        spread.start()
        return spread

    for part in range(PARTS):
        for year in range(2):
            returns(part, year)
        first_rates(part)
        if part == 0:
            advance(0, 0)
            t0 = totals(0)
            t0.start()
        else:
            t0.add_x()
            t0.add_z()
            advance(1, 0)
            t1 = totals(1)
            t1.start()
    for year in range(1, years):
        if year == 1:
            returns(0, 2)
        t1.add_x()
        s0 = declare(t0, year, 0)
        t1.add_z()
        if year == 1:
            returns(1, 2)
        s0.relay_z()
        s0.relay_x()
        s1 = declare(t1, year, 1)
        s0.finish()
        t0.settle()
        if year < years - 1:
            advance(0, year)
            t0 = totals(0)
            t0.start()
        s1.relay_z()
        if year < years - 1:
            t0.add_x()
        s1.relay_x()
        if year < years - 1:
            t0.add_z()
        s1.finish()
        t1.settle()
        if year < years - 1:
            advance(1, year)
            t1 = totals(1)
            t1.start()


def main(rows, tables, loadings, holdings, shocks, draws, size):
    secs, funds = holdings.shape
    years, factors, paths = shocks.shape
    count = rows[0].shape[1]
    depth = size // 4
    width = paths // PARTS
    own_rows = funds // size
    f32, bf16 = jnp.float32, jnp.bfloat16
    part = pltpu.VMEM((PARTS, depth, 2, own_rows, width), f32)
    vmem = pl.BlockSpec(memory_space=pltpu.VMEM)
    smem = pl.BlockSpec(memory_space=pltpu.SMEM)
    anywhere = pl.BlockSpec(memory_space=pl.ANY)
    dma = pltpu.SemaphoreType.DMA
    return pl.pallas_call(
        main_kernel,
        out_shape=(
            jax.ShapeDtypeStruct((PARTS, count, width), f32),
            jax.ShapeDtypeStruct((PARTS, count, width), f32),
            jax.ShapeDtypeStruct((years, PARTS, funds, width), f32),
            jax.ShapeDtypeStruct((years, PARTS, depth, 2, 2, own_rows, width), f32),
            jax.ShapeDtypeStruct((count, 2 * funds), bf16),
            jax.ShapeDtypeStruct((count, funds), f32),
        ),
        in_specs=[smem] * 2 + [vmem] * 8 + [anywhere] * 2,
        out_specs=(vmem,) * 6,
        scratch_shapes=[
            pltpu.VMEM((years, factors, paths), f32),
            pltpu.VMEM((years - 1, count, paths), bf16),
            pltpu.VMEM((2 * secs + 16, funds), f32),
            pltpu.VMEM((depth, 2, 2, 2 * secs + 16, funds), f32),
            pltpu.VMEM((depth, 4 * secs, 2 * factors), bf16),
            pltpu.VMEM((depth, 2 * funds, 4 * secs), bf16),
            pltpu.VMEM((years, funds, count), bf16),
            pltpu.VMEM((funds, funds), f32),
            pltpu.VMEM((PARTS, 2, depth, 2, 2, own_rows, width), f32),
            pltpu.VMEM((PARTS, depth, 2, 2, own_rows, width), f32),
            part,
            part,
            part,
            part,
            pltpu.VMEM((PARTS, own_rows, width), f32),
            dma((2,)),
            dma((2, 4 * depth)),
            dma((PARTS, 2, 4 * depth)),
            dma((PARTS, 2, 4 * depth)),
        ],
        compiler_params=pltpu.CompilerParams(
            collective_id=0, has_side_effects=True, vmem_limit_bytes=60 << 20
        ),
        name="project",
    )(*tables, *rows, loadings, holdings, shocks, draws)


def last_kernel(year, member, columns, assets, liability, fund_ret, rates, draws, held, owed):
    growth_of = stacked(fund_ret[...])
    credit_of = stacked(rates[...])
    for first in range(0, member.shape[0], ROWS):
        rows = slice(first, first + ROWS)
        held[rows], owed[rows] = year_step(
            member[rows],
            None,
            columns[rows, 4 + year : 5 + year],
            columns[rows, 1:2],
            columns[rows, 0:1],
            growth_of,
            credit_of,
            draws[rows],
            assets[rows],
            liability[rows],
        )


def last(member, columns, assets, liability, fund_ret, rates, draws):
    years, parts, funds, width = fund_ret.shape
    count = member.shape[0]
    inner = width // LANES
    state = pl.BlockSpec((None, count, LANES), lambda p, b: (p, 0, b))
    table = pl.BlockSpec((None, None, funds, LANES), lambda p, b: (years - 1, p, 0, b))
    out = pl.BlockSpec((count, LANES), lambda p, b: (0, p * inner + b))
    result = jax.ShapeDtypeStruct((count, parts * width), jnp.float32)
    return pl.pallas_call(
        functools.partial(last_kernel, years - 1),
        grid=(parts, inner),
        out_shape=(result, result),
        in_specs=[
            pl.BlockSpec(member.shape, lambda p, b: (0, 0)),
            pl.BlockSpec(columns.shape, lambda p, b: (0, 0)),
            state,
            state,
            table,
            table,
            pl.BlockSpec((None, count, LANES), lambda p, b: (years - 1, 0, p * inner + b)),
        ],
        out_specs=(out, out),
        name="last",
    )(member, columns, assets, liability, fund_ret, rates, draws)


def local(
    shocks,
    loadings,
    sec_drift,
    holdings,
    fund_of,
    product_type,
    term_years,
    asset_start,
    liab_start,
    base_lapse,
    guarantee,
    lapse_draw,
):
    years, _, paths = shocks.shape
    funds = holdings.shape[1]
    size = lax.axis_size("pol")
    vectors = (fund_of, product_type, term_years, asset_start, liab_start, sec_drift)
    rows = [vector.reshape(1, -1) for vector in vectors]
    draws = jnp.transpose(lapse_draw, (1, 0, 2))
    assets, liability, fund_ret, rates, member, columns = main(
        rows, (base_lapse, guarantee), loadings, holdings, shocks, draws, size
    )
    width = paths // PARTS
    rates = rates.reshape(years, PARTS, funds, width)
    assets, liability = last(member, columns, assets, liability, fund_ret, rates, draws)
    owned = paths // size
    first_path = lax.axis_index("pol") * owned
    mine = lax.dynamic_slice(
        rates, (0, first_path // width, 0, first_path % width), (years, 1, funds, owned)
    )
    return assets, liability, mine.reshape(years, funds, owned)


def solution(mesh):
    in_specs = (
        P("grp", None, None),
        P("pol", None),
        P("pol"),
        P("pol", None),
        P("pol", None),
        P("pol"),
        P("pol"),
        P("pol"),
        P("pol"),
        P(),
        P(),
        P("pol", "grp", None),
    )
    out_specs = (P("pol", "grp"), P("pol", "grp"), P("grp", None, "pol"))
    return jax.shard_map(local, mesh=mesh, in_specs=in_specs, out_specs=out_specs, check_vma=False)
```

time: 434 us -> 91.2 us (0.21)
  waiting for transfers between devices: 369 us -> 0 us
  Pallas kernels: 0 us -> 88.5 us
  matrix products: 34.8 us -> 0 us
  between operations: 14.1 us -> 0.65 us
  other arithmetic: 8.72 us -> 0 us
  local copies, waits for them, and re-layouts: 6.66 us -> 1.8 us
    psum x4 -> x0, waiting for transfers between devices: 369 us -> none  [the longest x3 272 us: local(): totals = lax.psum(fund_sums, 'pol')]
    pallas_call x0 -> x2, Pallas kernels: none -> 88.5 us  [the longest x1 82 us: main(): pl.pallas_call(main_kernel, out_shape=(jax.ShapeDtypeStruct((PARTS, count...]
    dot_general x14 -> x0, matrix products: 34.8 us -> none  [the longest x3 15.3 us: local(): jnp.dot(member, declared, precision=highest)]
    unnamed x38 -> x0, local copies, waits for them, and re-layouts: 5.43 us -> none
    add x3 -> x0, other arithmetic: 4.76 us -> none  [crediting(): return 0.01 + jax.nn.softplus(20.0 * (totals[0] / totals[1] - 1.05)) / 20.0]
  transfers between devices with their start and end apart: 4 -> 0, of which waited for: 4 -> 0; matrix products, arithmetic and copies ran while one was open for 2% -> 0% of each run, Pallas kernels for 0% -> 0%
where the time goes in v2:
time: 91.2 us; the launch traced here: 90.9 us
  Pallas kernels  88.5 us (97%)
  local copies, waits for them, and re-layouts  1.8 us (2%)
    pallas_call x1, Pallas kernels, main(): pl.pallas_call(main_kernel, out_shape=(jax.ShapeDtypeStruct((PARTS, count...  82 us
    pallas_call x1, Pallas kernels, last(): pl.pallas_call(functools.partial(last_kernel, years - 1), grid=(parts, in...  6.45 us

profile of v2, /device:TPU:0, one launch (start us, length us, event | category | flops | bytes accessed | tf_op | source)
XLA Modules:
  0.0 90.9 jit_solution(2529160761783320931)
XLA Ops:
  0.6 82.0 %project.1 = (f32[2,512,512]{2,1,0:T(8,128)}, f32[2,512,512]{2,1,0:T(8,128)}, f32[3,2,128,512]{3,2,1,0:T(8,128)}, f32[3,2,4,2,2,8,512]{6,5,4,3,2,1,0:T(8,128)}, ...) custom-call(f32[8]{0:T(128)} %base_lapse.1, f32[8]{0:T(128)} %guarantee.1, s32[1,512]{1,0:T(1,128)} %bitcast.14, ...), custom_call_target="tpu_custom_call" | custom-call | tf_op jit(solution)/shard_map/project/pallas_call | solution.py:442
  82.7 6.5 %last.1 = (f32[512,1024]{1,0:T(8,128)}, f32[512,1024]{1,0:T(8,128)}) custom-call(bf16[512,256]{1,0:T(8,128)(2,1)} %get-tuple-element.11.member, f32[512,128]{1,0:T(8,128)} %get-tuple-element.12.columns, f32[2,512,512]{2,1,0:T(8,128)} %get-tuple-element.13.assets, f32[2,512,512]{2,1,0:T(8,128)} %get-tuple-element.14.liability, ...), custom_call_target="tpu_custom_call" | custom-call | tf_op jit(solution)/shard_map/last/pallas_call | solution.py:509
  89.1 1.0 %constant_dynamic-slice_fusion = f32[3,1,128,64]{3,2,1,0:T(8,128)S(1)} fusion(f32[3,2,128,512]{3,2,1,0:T(8,128)} %bitcast.12, s32[]{:T(128)S(6)} %select_n.18, s32[]{:T(128)S(6)} %select_n.20), kind=kLoop, calls=%fused_computation | loop fusion | bytes 196616 | tf_op jit(solution)/shard_map/dynamic_slice | solution.py:555
  90.2 0.8 copy.15

commit v3 on v2

--- a/solution.py
+++ b/solution.py
@@ -12,6 +12,7 @@
 PARTS = 2
 LANES = 256
 ROWS = 256
+EARLY = 2
 
 
 def crediting(ra, rl):
@@ -87,29 +88,42 @@
         p, n = self.p, self.p.depth
         slot = self.every.at[p.z, p.x, p.core]
         self.along = [send(self.own, slot, self.sems, t, p.to_z(t)) for t in range(1, n)]
-        self.across = [send(self.own, slot, self.sems, n, p.to_x())]
-        self.pair = [send(self.own, slot, self.sems, 2 * n, p.to_core())]
+        self.across = {0: send(self.own, slot, self.sems, n, p.to_x())}
+        self.pair = {0: send(self.own, slot, self.sems, 2 * n, p.to_core())}
         self.every[p.z, p.x, p.core] = self.own[...]
 
+    def arrive_z(self, t):
+        p, n = self.p, self.p.depth
+        self.along[t - 1].wait_recv()
+        slot = self.every.at[p.behind(t), p.x, p.core]
+        self.across[t] = send(slot, slot, self.sems, n + t, p.to_x())
+        self.pair[t] = send(slot, slot, self.sems, 2 * n + t, p.to_core())
+
+    def arrive_x(self, t):
+        p, n = self.p, self.p.depth
+        self.across[t].wait_recv()
+        slot = self.every.at[p.behind(t), 1 - p.x, p.core]
+        self.pair[n + t] = send(slot, slot, self.sems, 3 * n + t, p.to_core())
+
+    def arrive_pair(self, t):
+        self.pair[t].wait_recv()
+        self.pair[self.p.depth + t].wait_recv()
+
     def relay_z(self):
-        p, n = self.p, self.p.depth
-        for t in range(1, n):
-            self.along[t - 1].wait_recv()
-            slot = self.every.at[p.behind(t), p.x, p.core]
-            self.across.append(send(slot, slot, self.sems, n + t, p.to_x()))
-            self.pair.append(send(slot, slot, self.sems, 2 * n + t, p.to_core()))
+        for t in range(1, self.p.depth):
+            self.arrive_z(t)
 
     def relay_x(self):
-        p, n = self.p, self.p.depth
-        for t in range(n):
-            self.across[t].wait_recv()
-            slot = self.every.at[p.behind(t), 1 - p.x, p.core]
-            self.pair.append(send(slot, slot, self.sems, 3 * n + t, p.to_core()))
+        for t in range(self.p.depth):
+            self.arrive_x(t)
 
     def finish(self):
-        for copy in self.pair:
-            copy.wait_recv()
-        for copy in self.along + self.across + self.pair:
+        for t in range(self.p.depth):
+            self.arrive_pair(t)
+        self.settle()
+
+    def settle(self):
+        for copy in self.along + list(self.across.values()) + list(self.pair.values()):
             copy.wait_send()
 
 
@@ -173,7 +187,7 @@
                 copy.wait_send()
 
 
-def year_step(member, hot, force, base, floor, growth_of, credit_of, draw, assets, liability):
+def year_step(member, force, base, floor, growth_of, credit_of, draw, assets, liability):
     growth = dot(member, growth_of)
     credit = jnp.maximum(dot(member, credit_of), floor)
     assets = assets * (1.0 + force * growth)
@@ -199,14 +213,18 @@
     draws_hbm,
     assets,
     liability,
+    mine,
     fund_ret,
     rates,
     member,
     columns,
     shocks,
+    pieces,
     draws,
     packed,
     every,
+    extra_own,
+    extra_every,
     loads,
     holds,
     hots,
@@ -220,6 +238,7 @@
     own,
     local_sems,
     gather_sems,
+    extra_sems,
     total_sems,
     spread_sems,
 ):
@@ -227,16 +246,19 @@
     secs, funds = holdings.shape
     count = fund_row.shape[1]
     years = shocks.shape[0]
-    width = assets.shape[2]
+    width = shocks.shape[2] // PARTS
     groups, group_secs, _ = loads.shape
     place = Place(depth)
 
     fetch_shocks = pltpu.make_async_copy(shocks_hbm, shocks, local_sems.at[0])
-    fetch_draws = pltpu.make_async_copy(
-        draws_hbm.at[pl.ds(0, years - 1)], draws, local_sems.at[1]
-    )
+    fetch_draws = pltpu.make_async_copy(draws_hbm, draws, local_sems.at[1])
     fetch_shocks.start()
     fetch_draws.start()
+    packed[:secs] = loadings[...]
+    packed[secs:] = holdings[...]
+    place.greet()
+    gather = Spread(place, packed, every, gather_sems)
+    gather.start()
 
     fund_id = lax.broadcasted_iota(jnp.int32, (funds, count), 0)
     hot = fund_row[...] == fund_id
@@ -260,55 +282,76 @@
     start_sums = jnp.dot(starts, member_f32, precision=HIGHEST)
     drifts = jnp.broadcast_to(drift_row[...], (8, secs))
     drift_sums = jnp.dot(drifts, holdings[...], precision=HIGHEST)
-    packed[:secs] = loadings[...]
-    packed[secs : 2 * secs] = holdings[...]
-    packed[2 * secs : 2 * secs + 8] = drift_sums
-    packed[2 * secs + 8 :] = start_sums
-
-    place.greet()
-    gather = Spread(place, packed, every, gather_sems)
-    gather.start()
-    narrow = member_f32.astype(jnp.bfloat16)
-    member[...] = jnp.concatenate([narrow, narrow], axis=1)
-    hots[0] = hot_rows.astype(jnp.bfloat16)
-    for year in range(1, years):
-        hots[year] = jnp.where(in_force[year] > 0.0, hot_rows, 0.0).astype(jnp.bfloat16)
-    gather.relay_z()
-    gather.relay_x()
-    gather.finish()
+    extra_own[:8] = drift_sums
+    extra_own[8:] = start_sums
+    extras = Spread(place, extra_own, extra_every, extra_sems)
+    extras.start()
     fetch_shocks.wait()
-    fetch_draws.wait()
-
-    per = group_secs // secs
-    flat = every.shape[0] * 4
-    extra = jnp.zeros((16, funds), jnp.float32)
-    for device in range(flat):
-        extra += every[device // 4, (device // 2) % 2, device % 2, 2 * secs :]
-    extra_columns[...] = jnp.concatenate(
-        [extra, jnp.zeros((funds - 16, funds), jnp.float32)], axis=0
-    ).T
-
-    def prepare(at, _):
+    for year in range(years):
+        for part in range(PARTS):
+            pieces[year, part] = stacked(shocks[year, :, part * width : (part + 1) * width])
+
+    def term_of(at, year, part):
+        exposure = dot(loads[at, :, : 2 * funds], pieces[year, part]) + dot(
+            loads[at, :, 2 * funds :], pieces[year, part, :funds]
+        )
+        t_high, t_low = split(0.25 * jnp.tanh(exposure))
+        both = dot(holds[at], t_high)
+        return both[:funds] + both[funds:] + dot(holds[at, :funds], t_low)
+
+    def compute(t):
+        at = place.behind(t)
         block = every[at]
         high, low = split(block[:, :, :secs].reshape(group_secs, funds))
-        loads[at] = jnp.concatenate([high, low], axis=1)
-        high, low = split(block[:, :, secs : 2 * secs].reshape(group_secs, funds).T)
+        loads[at] = jnp.concatenate([high, high, low], axis=1)
+        high, low = split(block[:, :, secs:].reshape(group_secs, funds).T)
         holds[at] = jnp.concatenate([high, low], axis=0)
-        return 0
-
-    lax.fori_loop(0, groups, prepare, 0)
+
+        def step(i, _):
+            year = i // PARTS
+            part = i - year * PARTS
+            term = term_of(at, year, part)
+            if t > 0:
+                term = term + fund_ret[year, part]
+            if t == depth - 1:
+                term = term + extra_columns[:, 0:1]
+            fund_ret[year, part] = term
+            return 0
+
+        lax.fori_loop(0, EARLY * PARTS, step, 0)
+
+    for t in range(depth):
+        if t + 1 < depth:
+            gather.arrive_z(t + 1)
+        gather.arrive_x(t)
+        if t == 0:
+            narrow = member_f32.astype(jnp.bfloat16)
+            member[...] = jnp.concatenate([narrow, narrow], axis=1)
+            hots[0] = hot_rows.astype(jnp.bfloat16)
+            for year in range(1, years):
+                hots[year] = jnp.where(in_force[year] > 0.0, hot_rows, 0.0).astype(jnp.bfloat16)
+        gather.arrive_pair(t)
+        if t == depth - 1:
+            extras.relay_z()
+            extras.relay_x()
+            extras.finish()
+            extra = jnp.zeros((16, funds), jnp.float32)
+            for device in range(4 * depth):
+                extra += extra_every[device // 4, (device // 2) % 2, device % 2]
+            extra_columns[...] = jnp.concatenate(
+                [extra, jnp.zeros((funds - 16, funds), jnp.float32)], axis=0
+            ).T
+        compute(t)
+    gather.settle()
+    fetch_draws.wait()
 
     def returns(part, year):
-        high, low = split(shocks[year, :, part * width : (part + 1) * width])
-        twice = jnp.concatenate([high, high], axis=0)
-
-        def step(at, total):
-            exposure = dot(loads[at], twice) + dot(loads[at, :, :funds], low)
-            t_high, t_low = split(0.25 * jnp.tanh(exposure))
-            both = dot(holds[at], t_high)
-            return total + both[:funds] + both[funds:] + dot(holds[at, :funds], t_low)
-
-        total = lax.fori_loop(0, groups, step, jnp.zeros((funds, width), jnp.float32))
+        total = lax.fori_loop(
+            0,
+            groups,
+            lambda at, total: total + term_of(at, year, part),
+            jnp.zeros((funds, width), jnp.float32),
+        )
         fund_ret[year, part] = total + extra_columns[:, 0:1]
 
     def first_rates(part):
@@ -320,6 +363,7 @@
     def advance(part, year):
         def step(block, _):
             lanes = pl.ds(pl.multiple_of(block * LANES, LANES), LANES)
+            whole = pl.ds(pl.multiple_of(part * width + block * LANES, LANES), LANES)
             growth_of = stacked(fund_ret[year, part, :, lanes])
             declared = rates[year, part, :, :, :, :, lanes].reshape(funds, LANES)
             credit_of = stacked(declared)
@@ -331,29 +375,31 @@
                     held = jnp.broadcast_to(columns[rows, 2:3], (ROWS, LANES))
                     owed = jnp.broadcast_to(columns[rows, 3:4], (ROWS, LANES))
                 else:
-                    held = assets[part, rows, lanes]
-                    owed = liability[part, rows, lanes]
-                draw_at = pl.ds(pl.multiple_of(part * width + block * LANES, LANES), LANES)
+                    held = assets[rows, whole]
+                    owed = liability[rows, whole]
                 held, owed = year_step(
                     member[rows],
-                    None,
                     columns[rows, 4 + year : 5 + year],
                     columns[rows, 1:2],
                     columns[rows, 0:1],
                     growth_of,
                     credit_of,
-                    draws[year, rows, draw_at],
+                    draws[year, rows, whole],
                     held,
                     owed,
                 )
-                assets[part, rows, lanes] = held
-                liability[part, rows, lanes] = owed
+                assets[rows, whole] = held
+                liability[rows, whole] = owed
+                if year == years - 1:
+                    continue
                 high, low = split(held)
                 pick = hots[year + 1, :, rows]
                 asset_sum += dot(pick, high) + dot(pick, low)
                 high, low = split(owed)
                 pick = hots[0, :, rows]
                 liab_sum += dot(pick, high) + dot(pick, low)
+            if year == years - 1:
+                return 0
             asset_sum = asset_sum * (1.0 + fund_ret[year + 1, part, :, lanes])
             shape = sums.shape[2:6] + (LANES,)
             sums[part, 0, :, :, :, :, lanes] = asset_sum.reshape(shape)
@@ -381,49 +427,59 @@
         spread.start()
         return spread
 
-    for part in range(PARTS):
-        for year in range(2):
-            returns(part, year)
-        first_rates(part)
-        if part == 0:
-            advance(0, 0)
-            t0 = totals(0)
-            t0.start()
-        else:
-            t0.add_x()
-            t0.add_z()
-            advance(1, 0)
-            t1 = totals(1)
-            t1.start()
+    first_rates(0)
+    advance(0, 0)
+    t0 = totals(0)
+    t0.start()
+    first_rates(1)
+    t0.add_x()
+    advance(1, 0)
+    t0.add_z()
+    t1 = totals(1)
+    t1.start()
     for year in range(1, years):
-        if year == 1:
-            returns(0, 2)
+        again = year < years - 1
         t1.add_x()
+        if year >= EARLY - 1 and again:
+            returns(0, year + 1)
         s0 = declare(t0, year, 0)
         t1.add_z()
-        if year == 1:
-            returns(1, 2)
+        if year >= EARLY - 1 and again:
+            returns(1, year + 1)
         s0.relay_z()
         s0.relay_x()
         s1 = declare(t1, year, 1)
         s0.finish()
         t0.settle()
-        if year < years - 1:
-            advance(0, year)
+        advance(0, year)
+        if again:
             t0 = totals(0)
             t0.start()
         s1.relay_z()
-        if year < years - 1:
+        if again:
             t0.add_x()
         s1.relay_x()
-        if year < years - 1:
+        if again:
             t0.add_z()
         s1.finish()
         t1.settle()
-        if year < years - 1:
-            advance(1, year)
+        advance(1, year)
+        if again:
             t1 = totals(1)
             t1.start()
+
+    owned = mine.shape[2]
+    first = lax.axis_index("pol") * owned
+    tile = min(width, 128)
+    inside = lax.rem(first, width)
+    start = pl.multiple_of((inside // tile) * tile, tile)
+    turn = lax.rem(inside, tile)
+    for year in range(years):
+        near = rates[year, first // width, :, :, :, :, pl.ds(start, tile)].reshape(funds, tile)
+        chosen = near[:, :owned]
+        for at in range(owned, tile, owned):
+            chosen = jnp.where(turn == at, near[:, at : at + owned], chosen)
+        mine[year] = chosen
 
 
 def main(rows, tables, loadings, holdings, shocks, draws, size):
@@ -442,21 +498,25 @@
     return pl.pallas_call(
         main_kernel,
         out_shape=(
-            jax.ShapeDtypeStruct((PARTS, count, width), f32),
-            jax.ShapeDtypeStruct((PARTS, count, width), f32),
-            jax.ShapeDtypeStruct((years, PARTS, funds, width), f32),
-            jax.ShapeDtypeStruct((years, PARTS, depth, 2, 2, own_rows, width), f32),
-            jax.ShapeDtypeStruct((count, 2 * funds), bf16),
-            jax.ShapeDtypeStruct((count, funds), f32),
+            jax.ShapeDtypeStruct((count, paths), f32),
+            jax.ShapeDtypeStruct((count, paths), f32),
+            jax.ShapeDtypeStruct((years, funds, paths // size), f32),
         ),
         in_specs=[smem] * 2 + [vmem] * 8 + [anywhere] * 2,
-        out_specs=(vmem,) * 6,
+        out_specs=(vmem,) * 3,
         scratch_shapes=[
+            pltpu.VMEM((years, PARTS, funds, width), f32),
+            pltpu.VMEM((years, PARTS, depth, 2, 2, own_rows, width), f32),
+            pltpu.VMEM((count, 2 * funds), bf16),
+            pltpu.VMEM((count, funds), f32),
             pltpu.VMEM((years, factors, paths), f32),
-            pltpu.VMEM((years - 1, count, paths), bf16),
-            pltpu.VMEM((2 * secs + 16, funds), f32),
-            pltpu.VMEM((depth, 2, 2, 2 * secs + 16, funds), f32),
-            pltpu.VMEM((depth, 4 * secs, 2 * factors), bf16),
+            pltpu.VMEM((years, PARTS, 2 * factors, width), bf16),
+            pltpu.VMEM((years, count, paths), bf16),
+            pltpu.VMEM((2 * secs, funds), f32),
+            pltpu.VMEM((depth, 2, 2, 2 * secs, funds), f32),
+            pltpu.VMEM((16, funds), f32),
+            pltpu.VMEM((depth, 2, 2, 16, funds), f32),
+            pltpu.VMEM((depth, 4 * secs, 3 * factors), bf16),
             pltpu.VMEM((depth, 2 * funds, 4 * secs), bf16),
             pltpu.VMEM((years, funds, count), bf16),
             pltpu.VMEM((funds, funds), f32),
@@ -469,6 +529,7 @@
             pltpu.VMEM((PARTS, own_rows, width), f32),
             dma((2,)),
             dma((2, 4 * depth)),
+            dma((2, 4 * depth)),
             dma((PARTS, 2, 4 * depth)),
             dma((PARTS, 2, 4 * depth)),
         ],
@@ -477,51 +538,6 @@
         ),
         name="project",
     )(*tables, *rows, loadings, holdings, shocks, draws)
-
-
-def last_kernel(year, member, columns, assets, liability, fund_ret, rates, draws, held, owed):
-    growth_of = stacked(fund_ret[...])
-    credit_of = stacked(rates[...])
-    for first in range(0, member.shape[0], ROWS):
-        rows = slice(first, first + ROWS)
-        held[rows], owed[rows] = year_step(
-            member[rows],
-            None,
-            columns[rows, 4 + year : 5 + year],
-            columns[rows, 1:2],
-            columns[rows, 0:1],
-            growth_of,
-            credit_of,
-            draws[rows],
-            assets[rows],
-            liability[rows],
-        )
-
-
-def last(member, columns, assets, liability, fund_ret, rates, draws):
-    years, parts, funds, width = fund_ret.shape
-    count = member.shape[0]
-    inner = width // LANES
-    state = pl.BlockSpec((None, count, LANES), lambda p, b: (p, 0, b))
-    table = pl.BlockSpec((None, None, funds, LANES), lambda p, b: (years - 1, p, 0, b))
-    out = pl.BlockSpec((count, LANES), lambda p, b: (0, p * inner + b))
-    result = jax.ShapeDtypeStruct((count, parts * width), jnp.float32)
-    return pl.pallas_call(
-        functools.partial(last_kernel, years - 1),
-        grid=(parts, inner),
-        out_shape=(result, result),
-        in_specs=[
-            pl.BlockSpec(member.shape, lambda p, b: (0, 0)),
-            pl.BlockSpec(columns.shape, lambda p, b: (0, 0)),
-            state,
-            state,
-            table,
-            table,
-            pl.BlockSpec((None, count, LANES), lambda p, b: (years - 1, 0, p * inner + b)),
-        ],
-        out_specs=(out, out),
-        name="last",
-    )(member, columns, assets, liability, fund_ret, rates, draws)
 
 
 def local(
@@ -538,24 +554,11 @@
     guarantee,
     lapse_draw,
 ):
-    years, _, paths = shocks.shape
-    funds = holdings.shape[1]
     size = lax.axis_size("pol")
     vectors = (fund_of, product_type, term_years, asset_start, liab_start, sec_drift)
     rows = [vector.reshape(1, -1) for vector in vectors]
     draws = jnp.transpose(lapse_draw, (1, 0, 2))
-    assets, liability, fund_ret, rates, member, columns = main(
-        rows, (base_lapse, guarantee), loadings, holdings, shocks, draws, size
-    )
-    width = paths // PARTS
-    rates = rates.reshape(years, PARTS, funds, width)
-    assets, liability = last(member, columns, assets, liability, fund_ret, rates, draws)
-    owned = paths // size
-    first_path = lax.axis_index("pol") * owned
-    mine = lax.dynamic_slice(
-        rates, (0, first_path // width, 0, first_path % width), (years, 1, funds, owned)
-    )
-    return assets, liability, mine.reshape(years, funds, owned)
+    return main(rows, (base_lapse, guarantee), loadings, holdings, shocks, draws, size)
 
 
 def solution(mesh):

time: 91.2 us -> 85.4 us (0.936)
  Pallas kernels: 88.5 us -> 78.2 us
  local copies, waits for them, and re-layouts: 1.8 us -> 6.31 us
    pallas_call x2 -> x1, Pallas kernels: 88.5 us -> 78.2 us  [main(): pl.pallas_call(main_kernel, out_shape=(jax.ShapeDtypeStruct((count, paths...]
    unnamed x0 -> x4, local copies, waits for them, and re-layouts: none -> 4.63 us
    dynamic_slice x2 -> x0, local copies, waits for them, and re-layouts: 1.8 us -> none  [local(): lax.dynamic_slice(rates, (0, first_path // width, 0, first_path % width),...]
    pallas_call x0 -> x1, local copies, waits for them, and re-layouts: none -> 1.68 us  [main(): pl.pallas_call(main_kernel, out_shape=(jax.ShapeDtypeStruct((count, paths...]
where the time goes in v3:
time: 85.4 us; the launch traced here: 85.2 us
  Pallas kernels  78.2 us (92%)
  local copies, waits for them, and re-layouts  6.31 us (7%)
    pallas_call x1, Pallas kernels, main(): pl.pallas_call(main_kernel, out_shape=(jax.ShapeDtypeStruct((count, paths...  78.2 us
    unnamed x4, local copies, waits for them, and re-layouts  4.63 us

profile of v3, /device:TPU:0, one launch (start us, length us, event | category | flops | bytes accessed | tf_op | source)
XLA Modules:
  0.0 85.2 jit_solution(8275729778464319145)
XLA Ops:
  0.6 78.2 %project.1 = (f32[512,1024]{1,0:T(8,128)}, f32[512,1024]{1,0:T(8,128)}, f32[3,128,64]{2,1,0:T(8,128)}) custom-call(f32[8]{0:T(128)} %base_lapse.1, f32[8]{0:T(128)} %guarantee.1, s32[1,512]{1,0:T(1,128)} %bitcast.8, s32[1,512]{1,0:T(1,128)} %bitcast.9, s32[1,512]{1,0:T(1,128)} %bitcast.10, f32[1,512]{1,0:T(1,128)} %bitcast.11, f32[1,512]{1,0:T(1,128)} %bitcast.12, ...), custom_call_target="tpu_custom_call" | custom-call | tf_op jit(solution)/shard_map/project/pallas_call | solution.py:498
  78.9 1.7 %copy.15 = f32[3,128,64]{1,2,0:T(8,128)} copy(f32[3,128,64]{2,1,0:T(8,128)} %get-tuple-element.5) | data formatting | bytes 196608 | tf_op jit(solution)/shard_map/project/pallas_call | solution.py:498
  80.6 0.0 copy-start
  80.6 3.3 %copy.18 = f32[512,1024]{1,0:T(8,128)} copy(f32[512,1024]{1,0:T(8,128)} %get-tuple-element.9) | data formatting | bytes 4194304
  83.9 0.0 copy-done
  83.9 1.3 %copy.19 = f32[512,1024]{1,0:T(8,128)} copy(f32[512,1024]{1,0:T(8,128)S(1)} %copy-done) | data formatting | bytes 4194304
Async XLA Ops:
  80.6 3.3 %copy-start = (f32[512,1024]{1,0:T(8,128)S(1)}, f32[512,1024]{1,0:T(8,128)}, u32[]{:S(2)}) copy-start(f32[512,1024]{1,0:T(8,128)} %get-tuple-element.10) | copy-start | bytes 6291460
